TPU v7x, 512 devices: a whole 4x4x16 slice. The times are simulated.
512 devices in a mesh: row: 32 (over y, z_hi, x), col: 16 (over z_lo, core).
Axes of the slice: x: 4, y: 4, z: 16 (z_hi: 2, z_lo: 8; z = z_hi * 8 + z_lo), core: 2. Of those that a mesh axis runs over, the one named last changes fastest.
Arguments:
- query_field: bfloat16 [512, 256, 1152], P('row', 'col'), may hold values from -136 to 136
- key_field: bfloat16 [512, 256, 1152], P('row', 'col'), may hold values from -8.5 to 8.5
- value_field: bfloat16 [512, 256, 1152], P('row', 'col'), may hold values from -6 to 6
- query_tan: bfloat16 [512, 256, 1152], P('row', 'col'), may hold values from -6 to 6
- key_tan: bfloat16 [512, 256, 1152], P('row', 'col'), may hold values from -6 to 6
- value_tan: bfloat16 [512, 256, 1152], P('row', 'col'), may hold values from -6 to 6
- pool_near: float32 [4, 4], replicated, may hold values from -1.5 to 1.5
- pool_far: float32 [16, 16], replicated, may hold values from -0.375 to 0.375
- level_bias: float32 [2, 16], replicated, may hold values from 0.5 to 2.5
Outputs:
- mixed: bfloat16 [512, 256, 1152], P('row', 'col')
- mixed_tan: bfloat16 [512, 256, 1152], P('row', 'col')
All inputs are finite; a program needn't handle non-finite values.
Results may differ from a plain program's by a relative error of at most 0.012.
Values may be sent and summed in bfloat16 or wider, within the bound.
A program may use at most 128 MiB of HBM per device.

v0:
```python
import jax
import jax.numpy as jnp
from jax import lax
from jax.sharding import PartitionSpec as P

HEADS = 16
RIM = 8
NEAR_POOL = 4


def with_halo(cells, sides, width):
    for axis, dim in sides:
        count = lax.axis_size(axis)
        ends = count - 1
        head = lax.slice_in_dim(cells, 0, width, axis=dim)
        tail = lax.slice_in_dim(cells, cells.shape[dim] - width, cells.shape[dim], axis=dim)
        cells = jnp.concatenate(
            [
                lax.ppermute(tail, axis, [(i, (i + 1) % count) for i in range(ends)]),
                cells,
                lax.ppermute(head, axis, [((i + 1) % count, i) for i in range(ends)]),
            ],
            axis=dim,
        )
    return cells


def partner(block, axis, stride):
    count = lax.axis_size(axis)
    route = []
    for low in range(count):
        high = low | 1 << stride
        if high != low and high < count:
            route += [(low, high), (high, low)]
    return lax.ppermute(block, axis, route)


def pool_stack(stacked_wide, weights, size):
    count, row_count, col_count, width = stacked_wide.shape
    blocks = stacked_wide.reshape(count, row_count // size, size, col_count // size, size, width)
    pooled = jnp.einsum("napbqd,pq->nabd", blocks, weights, precision=lax.Precision.HIGHEST)
    return pooled.astype(jnp.bfloat16).reshape(count, -1, width)


def body(
    query_field,
    key_field,
    value_field,
    query_tan,
    key_tan,
    value_tan,
    pool_near,
    pool_far,
    level_bias,
):
    window = query_field.shape[0]
    width = query_field.shape[2]
    head_dim = width // HEADS
    pair_width = 2 * head_dim
    token_count = window * window
    score_scale = head_dim ** (-0.5)
    stacked = jnp.stack([key_field, value_field, key_tan, value_tan], 0)
    extended = with_halo(stacked, (("row", 1), ("col", 2)), RIM)
    span = window + 2 * RIM
    fine_keys = extended.reshape(4, span * span, width)
    stacked_wide = stacked.astype(jnp.float32)
    near_local = pool_stack(stacked_wide, pool_near, NEAR_POOL)
    near_pair = jnp.concatenate([near_local, partner(near_local, "row", 0)], axis=1)
    near_keys = jnp.concatenate([near_pair, partner(near_pair, "col", 0)], axis=1)
    far_local = pool_stack(stacked_wide, pool_far, window)
    col_done = lax.all_gather(far_local, "col", axis=1, tiled=True)
    far_keys = lax.all_gather(col_done, "row", axis=1, tiled=True)
    row_ids = lax.axis_index("row") * window - RIM + jnp.arange(span, dtype=jnp.int32)
    col_ids = lax.axis_index("col") * window - RIM + jnp.arange(span, dtype=jnp.int32)
    row_ok = (row_ids >= 0) & (row_ids < window * lax.axis_size("row"))
    col_ok = (col_ids >= 0) & (col_ids < window * lax.axis_size("col"))
    valid = (row_ok[:, None] & col_ok[None, :]).reshape(span * span)
    query_flat = query_field.reshape(token_count, width)
    qtan_flat = query_tan.reshape(token_count, width)
    blocks = (fine_keys, near_keys, far_keys)

    def pair_step(group, carry):
        out_acc, tan_acc = carry
        start = group * pair_width

        def columns(array):
            return lax.dynamic_slice_in_dim(array, start, pair_width, array.ndim - 1)

        query_pair = columns(query_flat).reshape(token_count, 2, head_dim)
        qtan_pair = columns(qtan_flat).reshape(token_count, 2, head_dim)
        bias_pair = lax.dynamic_slice_in_dim(level_bias, group * 2, 2, 1)
        score_parts = []
        tangent_parts = []
        value_parts = []
        valtan_parts = []
        for level, block in enumerate(blocks):
            count = block.shape[1]
            key_part = columns(block[0]).reshape(count, 2, head_dim)
            keytan_part = columns(block[2]).reshape(count, 2, head_dim)
            value_parts.append(columns(block[1]).reshape(count, 2, head_dim))
            valtan_parts.append(columns(block[3]).reshape(count, 2, head_dim))
            level_scores = (
                jnp.einsum("qhd,khd->hqk", query_pair, key_part, preferred_element_type=jnp.float32)
                * score_scale
            )
            if level == 0:
                level_scores = jnp.where(valid[None, None, :], level_scores, jnp.float32(-jnp.inf))
            else:
                level_scores = level_scores + bias_pair[level - 1][:, None, None]
            score_parts.append(level_scores)
            tangent_parts.append(
                (
                    jnp.einsum(
                        "qhd,khd->hqk", qtan_pair, key_part, preferred_element_type=jnp.float32
                    )
                    + jnp.einsum(
                        "qhd,khd->hqk", query_pair, keytan_part, preferred_element_type=jnp.float32
                    )
                )
                * score_scale
            )
        top = jnp.max(score_parts[0], axis=-1, keepdims=True)
        for level in range(1, 3):
            top = jnp.maximum(top, jnp.max(score_parts[level], axis=-1, keepdims=True))
        total = jnp.zeros_like(top)
        for level in range(3):
            total = total + jnp.sum(jnp.exp(score_parts[level] - top), axis=-1, keepdims=True)
        row_total = jnp.zeros((2, token_count), jnp.float32)
        mix = jnp.zeros((token_count, 2, head_dim), jnp.float32)
        mix_extra = jnp.zeros((token_count, 2, head_dim), jnp.float32)
        for level in range(3):
            weights = jnp.exp(score_parts[level] - top) / total
            product = weights * tangent_parts[level]
            row_total = row_total + jnp.sum(product, axis=-1)
            weight_part = weights.astype(jnp.bfloat16)
            product_part = product.astype(jnp.bfloat16)
            mix = mix + jnp.einsum(
                "hqk,khd->qhd", weight_part, value_parts[level], preferred_element_type=jnp.float32
            )
            mix_extra = mix_extra + jnp.einsum(
                "hqk,khd->qhd", product_part, value_parts[level], preferred_element_type=jnp.float32
            )
            mix_extra = mix_extra + jnp.einsum(
                "hqk,khd->qhd", weight_part, valtan_parts[level], preferred_element_type=jnp.float32
            )
        mix_tan = mix_extra - jnp.transpose(row_total)[:, :, None] * mix
        out_acc = lax.dynamic_update_slice_in_dim(
            out_acc, mix.reshape(token_count, pair_width).astype(jnp.bfloat16), start, 1
        )
        tan_acc = lax.dynamic_update_slice_in_dim(
            tan_acc, mix_tan.reshape(token_count, pair_width).astype(jnp.bfloat16), start, 1
        )
        return (out_acc, tan_acc)

    empty = jnp.zeros((token_count, width), jnp.bfloat16)
    mixed, mixed_tan = lax.fori_loop(0, HEADS // 2, pair_step, (empty, empty))
    return (mixed.reshape(window, window, width), mixed_tan.reshape(window, window, width))


def solution(mesh):
    in_specs = (
        P("row", "col", None),
        P("row", "col", None),
        P("row", "col", None),
        P("row", "col", None),
        P("row", "col", None),
        P("row", "col", None),
        P(),
        P(),
        P(),
    )
    out_specs = (P("row", "col", None), P("row", "col", None))
    return jax.shard_map(body, mesh=mesh, in_specs=in_specs, out_specs=out_specs, check_vma=False)
```

profile of v0, /device:TPU:25, one launch (start us, length us, event | category | flops | bytes accessed | tf_op | source)
XLA Modules:
  0.0 472.6 jit_solution(2326812249168049933)
XLA Ops:
  10.9 3.3 collective-permute-start
  14.1 16.6 %collective-permute-start.1 = (bf16[4,8,16,1152]{3,2,1,0:T(8,128)(2,1)}, bf16[4,8,16,1152]{3,2,1,0:T(8,128)(2,1)}, u32[]{:S(2)}, u32[]{:S(2)}) collective-permute-start(bf16[4,8,16,1152]{3,2,1,0:T(8,128)(2,1)} %get-tuple-element.266), channel_id=1, source_target_pairs={{16,0},{32,16},{48,32},{64,48},{80,64},{96,80},{112,96},{128,112},... | collective-permute-start | bytes 3538952 | tf_op jit(solution)/shard_map/ppermute | solution.py:21
  31.9 124.5 %all-gather = bf16[4,18432]{1,0:T(4,128)(2,1)S(1)} all-gather(bf16[4,1152]{1,0:T(4,128)(2,1)S(1)} %bitcast.210), channel_id=2, replica_groups=mesh['row'=32,'col'=16] {'col'}, dimensions={1}, use_global_device_ids=true | all-gather | bytes 156672 | tf_op jit(solution)/shard_map/all_gather | solution.py:71
  157.1 2.8 pad_maximum_fusion.1
  160.0 2.6 fusion.55
  164.5 3.9 collective-permute-start.3
  170.6 3.6 fusion.44
  176.3 5.8 %collective-permute-done.4 = bf16[4,16,1152]{2,1,0:T(8,128)(2,1)S(1)} collective-permute-done((bf16[4,16,1152]{2,1,0:T(8,128)(2,1)S(1)}, bf16[4,16,1152]{2,1,0:T(8,128)(2,1)S(1)}, u32[]{:S(2)}, u32[]{:S(2)}) %collective-permute-start.4) | collective-permute-done | bytes 147488 | tf_op jit(solution)/shard_map/ppermute | solution.py:35
  182.1 2.2 collective-permute-start.5
  189.0 5.8 %collective-permute-done.2 = bf16[4,32,8,1152]{3,2,1,0:T(8,128)(2,1)} collective-permute-done((bf16[4,32,8,1152]{3,2,1,0:T(8,128)(2,1)}, bf16[4,32,8,1152]{3,2,1,0:T(8,128)(2,1)}, u32[]{:S(2)}, u32[]{:S(2)}) %collective-permute-start.2) | collective-permute-done | bytes 2359328 | tf_op jit(solution)/shard_map/ppermute | solution.py:19
  194.8 4.4 collective-permute-done.3
  199.2 9.8 %pad_maximum_fusion = bf16[4,32,32,1152]{3,2,1,0:T(8,128)(2,1)} fusion(bf16[4,32,8,1152]{3,2,1,0:T(8,128)(2,1)} %collective-permute-done.3, bf16[4,8,16,1152]{3,2,1,0:T(8,128)(2,1)} %collective-permute-done.1, bf16[1,16,16,1152]{3,2,1,0:T(8,128)(2,1)S(1)} %bitcast.188, bf16[1,16,16,1152]{3,2,1,0:T(8,128)(2,1)S(1)} %bitcast.191, ...), kind=kLoop, calls=%fused_computation.75 | loop fusion | flops 75497472 | bytes 18874368 | tf_op jit(solution)/shard_map/concatenate | solution.py:17
  209.0 12.6 %copy.22 = bf16[4,1024,1152]{1,2,0:T(8,128)(2,1)} copy(bf16[4,1024,1152]{2,1,0:T(8,128)(2,1)} %bitcast.169) | data formatting | bytes 18874368
  221.6 106.0 %all-gather.3.cloned.1.call-done = bf16[4,512,1152]{2,1,0:T(8,128)(2,1)} async-done(((bf16[4,16,1152]{2,1,0:T(8,128)(2,1)}), bf16[4,512,1152]{2,1,0:T(8,128)(2,1)}) %all-gather.3.cloned.1.call-update) | async-done | bytes 4718608 | tf_op jit(solution)/shard_map/all_gather | solution.py:72
  327.6 6.7 %copy.24 = bf16[4,512,1152]{1,2,0:T(8,128)(2,1)} copy(bf16[4,512,1152]{2,1,0:T(8,128)(2,1)} %all-gather.3.cloned.1.call-done) | data formatting | bytes 9437184
  334.4 129.2 %while.16 = (s32[]{:T(128)}, bf16[256,1152]{0,1:T(8,128)(2,1)S(1)}, bf16[256,1152]{0,1:T(8,128)(2,1)S(1)}, bf16[4,1024,1152]{1,2,0:T(8,128)(2,1)}, bf16[256,1152...) while((s32[]{:T(128)}, bf16[256,1152]{0,1:T(8,128)(2,1)S(1)}, ...), condition=%wide.region_10.11_spmd.clone, body=%wide.region_0.10_spmd.clone.sunk | while | flops 726347264 | bytes 104430016 | solution.py:156
  336.7 2.8 fusion.181
  352.8 2.8 fusion.181
  369.0 2.8 fusion.181
  385.2 2.8 fusion.181
  401.3 2.8 fusion.181
  417.5 2.8 fusion.181
  433.6 2.8 fusion.181
  449.8 2.8 fusion.181
  (463 shorter events, 123.5 us)
Async XLA Ops:
  7.2 23.6 %copy-start = (f32[16,16]{1,0:T(8,128)S(1)}, f32[16,16]{1,0:T(8,128)}, u32[]{:S(2)}) copy-start(f32[16,16]{1,0:T(8,128)} %param.18) | copy-start | bytes 3076
  7.2 320.5 %all-gather.3.cloned.1.call-start = ((), (), s32[]{:S(2)}) async-start(), calls=%async_computation | async-start | bytes 4866048 | tf_op jit(solution)/shard_map/all_gather | solution.py:72
  10.8 146.2 %copy-start.3 = (bf16[16,16,1152]{2,1,0:T(8,128)(2,1)S(1)}, bf16[16,16,1152]{2,1,0:T(8,128)(2,1)}, u32[]{:S(2)}) copy-start(bf16[16,16,1152]{2,1,0:T(8,128)(2,1)} %param.16) | copy-start | bytes 1769476
  10.8 146.2 %copy-start.4 = (bf16[16,16,1152]{2,1,0:T(8,128)(2,1)S(1)}, bf16[16,16,1152]{2,1,0:T(8,128)(2,1)}, u32[]{:S(2)}) copy-start(bf16[16,16,1152]{2,1,0:T(8,128)(2,1)} %param.15) | copy-start | bytes 1769476
  10.9 146.3 %copy-start.5 = (bf16[16,16,1152]{2,1,0:T(8,128)(2,1)S(1)}, bf16[16,16,1152]{2,1,0:T(8,128)(2,1)}, u32[]{:S(2)}) copy-start(bf16[16,16,1152]{2,1,0:T(8,128)(2,1)} %param.13) | copy-start | bytes 1769476
  10.9 146.3 %copy-start.6 = (bf16[16,16,1152]{2,1,0:T(8,128)(2,1)S(1)}, bf16[16,16,1152]{2,1,0:T(8,128)(2,1)}, u32[]{:S(2)}) copy-start(bf16[16,16,1152]{2,1,0:T(8,128)(2,1)} %param.12) | copy-start | bytes 1769476
  10.9 146.2 %collective-permute-start = (bf16[4,8,16,1152]{3,2,1,0:T(8,128)(2,1)}, bf16[4,8,16,1152]{3,2,1,0:T(8,128)(2,1)}, u32[]{:S(2)}, u32[]{:S(2)}) collective-permute-start(bf16[4,8,16,1152]{3,2,1,0:T(8,128)(2,1)} %get-tuple-element.265), channel_id=1, source_target_pairs={{0,16},{16,32},{32,48},{48,64},{64,80},{80,96},{96,112},{112,128},... | collective-permute-start | bytes 3538952 | tf_op jit(solution)/shard_map/ppermute | solution.py:19
  14.1 143.0 %collective-permute-start.1 = (bf16[4,8,16,1152]{3,2,1,0:T(8,128)(2,1)}, bf16[4,8,16,1152]{3,2,1,0:T(8,128)(2,1)}, u32[]{:S(2)}, u32[]{:S(2)}) collective-permute-start(bf16[4,8,16,1152]{3,2,1,0:T(8,128)(2,1)} %get-tuple-element.266), channel_id=1, source_target_pairs={{16,0},{32,16},{48,32},{64,48},{80,64},{96,80},{112,96},{128,112},... | collective-permute-start | bytes 3538952 | tf_op jit(solution)/shard_map/ppermute | solution.py:21
  162.6 32.2 %collective-permute-start.2 = (bf16[4,32,8,1152]{3,2,1,0:T(8,128)(2,1)}, bf16[4,32,8,1152]{3,2,1,0:T(8,128)(2,1)}, u32[]{:S(2)}, u32[]{:S(2)}) collective-permute-start(bf16[4,32,8,1152]{3,2,1,0:T(8,128)(2,1)} %get-tuple-element.263), channel_id=1, source_target_pairs={{0,1},{1,2},{2,3},{3,4},{4,5},{5,6},{6,7},{7,8},{8,9},{9,10},{10,1... | collective-permute-start | bytes 7077896 | tf_op jit(solution)/shard_map/ppermute | solution.py:19
  164.5 6.1 %copy-start.10 = (f32[4,4]{1,0:T(4,128)S(1)}, f32[4,4]{1,0:T(4,128)}, u32[]{:S(2)}) copy-start(f32[4,4]{1,0:T(4,128)} %param.17) | copy-start | bytes 196
  164.5 34.7 %collective-permute-start.3 = (bf16[4,32,8,1152]{3,2,1,0:T(8,128)(2,1)}, bf16[4,32,8,1152]{3,2,1,0:T(8,128)(2,1)}, u32[]{:S(2)}, u32[]{:S(2)}) collective-permute-start(bf16[4,32,8,1152]{3,2,1,0:T(8,128)(2,1)} %get-tuple-element.264), channel_id=1, source_target_pairs={{1,0},{2,1},{3,2},{4,3},{5,4},{6,5},{7,6},{8,7},{9,8},{10,9},{11,1... | collective-permute-start | bytes 7077896 | tf_op jit(solution)/shard_map/ppermute | solution.py:21
  174.3 13.5 %copy-start.7 = (bf16[4,16,1152]{2,1,0:T(8,128)(2,1)}, bf16[4,16,1152]{2,1,0:T(8,128)(2,1)S(1)}, u32[]{:S(2)}) copy-start(bf16[4,16,1152]{2,1,0:T(8,128)(2,1)S(1)} %reshape.226) | copy-start | bytes 442372
  174.3 7.8 %collective-permute-start.4 = (bf16[4,16,1152]{2,1,0:T(8,128)(2,1)S(1)}, bf16[4,16,1152]{2,1,0:T(8,128)(2,1)S(1)}, u32[]{:S(2)}, u32[]{:S(2)}) collective-permute-start(bf16[4,16,1152]{2,1,0:T(8,128)(2,1)S(1)} %reshape.226), channel_id=1, source_target_pairs={{0,16},{16,0},{32,48},{48,32},{64,80},{80,64},{96,112},{112,96},{1... | collective-permute-start | bytes 442376 | tf_op jit(solution)/shard_map/ppermute | solution.py:35
  182.1 5.7 %copy-start.8 = (bf16[4,16,1152]{2,1,0:T(8,128)(2,1)}, bf16[4,16,1152]{2,1,0:T(8,128)(2,1)S(1)}, u32[]{:S(2)}) copy-start(bf16[4,16,1152]{2,1,0:T(8,128)(2,1)S(1)} %collective-permute-done.4) | copy-start | bytes 442372
  182.1 5.7 %collective-permute-start.5 = (bf16[4,32,1152]{2,1,0:T(8,128)(2,1)S(1)}, bf16[4,32,1152]{2,1,0:T(8,128)(2,1)}, u32[]{:S(2)}, u32[]{:S(2)}) collective-permute-start(bf16[4,32,1152]{2,1,0:T(8,128)(2,1)S(1)} %pad_maximum_fusion.8), channel_id=1, source_target_pairs={{0,1},{1,0},{2,3},{3,2},{4,5},{5,4},{6,7},{7,6},{8,9},{9,8},{10,11... | collective-permute-start | bytes 884744 | tf_op jit(solution)/shard_map/ppermute | solution.py:35
  221.6 112.8 %copy-start.9 = (f32[2,16]{1,0:T(2,128)S(1)}, f32[2,16]{1,0:T(2,128)}, u32[]{:S(2)}) copy-start(f32[2,16]{1,0:T(2,128)} %param.19) | copy-start | bytes 388
  336.7 5.1 %copy-start.2 = (bf16[4,1024,1152]{1,2,0:T(8,128)(2,1)S(1)}, bf16[4,1024,1152]{1,2,0:T(8,128)(2,1)}, u32[]{:S(2)}) copy-start(bf16[4,1024,1152]{1,2,0:T(8,128)(2,1)} %get-tuple-element.439) | copy-start | bytes 28311556 | tf_op jit(solution)/shard_map/while
  352.8 5.1 %copy-start.2 = (bf16[4,1024,1152]{1,2,0:T(8,128)(2,1)S(1)}, bf16[4,1024,1152]{1,2,0:T(8,128)(2,1)}, u32[]{:S(2)}) copy-start(bf16[4,1024,1152]{1,2,0:T(8,128)(2,1)} %get-tuple-element.439) | copy-start | bytes 28311556 | tf_op jit(solution)/shard_map/while
  369.0 5.1 %copy-start.2 = (bf16[4,1024,1152]{1,2,0:T(8,128)(2,1)S(1)}, bf16[4,1024,1152]{1,2,0:T(8,128)(2,1)}, u32[]{:S(2)}) copy-start(bf16[4,1024,1152]{1,2,0:T(8,128)(2,1)} %get-tuple-element.439) | copy-start | bytes 28311556 | tf_op jit(solution)/shard_map/while
  385.1 5.1 %copy-start.2 = (bf16[4,1024,1152]{1,2,0:T(8,128)(2,1)S(1)}, bf16[4,1024,1152]{1,2,0:T(8,128)(2,1)}, u32[]{:S(2)}) copy-start(bf16[4,1024,1152]{1,2,0:T(8,128)(2,1)} %get-tuple-element.439) | copy-start | bytes 28311556 | tf_op jit(solution)/shard_map/while
  401.3 5.1 %copy-start.2 = (bf16[4,1024,1152]{1,2,0:T(8,128)(2,1)S(1)}, bf16[4,1024,1152]{1,2,0:T(8,128)(2,1)}, u32[]{:S(2)}) copy-start(bf16[4,1024,1152]{1,2,0:T(8,128)(2,1)} %get-tuple-element.439) | copy-start | bytes 28311556 | tf_op jit(solution)/shard_map/while
  417.4 5.1 %copy-start.2 = (bf16[4,1024,1152]{1,2,0:T(8,128)(2,1)S(1)}, bf16[4,1024,1152]{1,2,0:T(8,128)(2,1)}, u32[]{:S(2)}) copy-start(bf16[4,1024,1152]{1,2,0:T(8,128)(2,1)} %get-tuple-element.439) | copy-start | bytes 28311556 | tf_op jit(solution)/shard_map/while
  433.6 5.1 %copy-start.2 = (bf16[4,1024,1152]{1,2,0:T(8,128)(2,1)S(1)}, bf16[4,1024,1152]{1,2,0:T(8,128)(2,1)}, u32[]{:S(2)}) copy-start(bf16[4,1024,1152]{1,2,0:T(8,128)(2,1)} %get-tuple-element.439) | copy-start | bytes 28311556 | tf_op jit(solution)/shard_map/while
  449.7 5.1 %copy-start.2 = (bf16[4,1024,1152]{1,2,0:T(8,128)(2,1)S(1)}, bf16[4,1024,1152]{1,2,0:T(8,128)(2,1)}, u32[]{:S(2)}) copy-start(bf16[4,1024,1152]{1,2,0:T(8,128)(2,1)} %get-tuple-element.439) | copy-start | bytes 28311556 | tf_op jit(solution)/shard_map/while
  (1 other events, 2.1 us)
Sparse Core Ops, SparseCore 0:
  157.2 170.4 all-gather.2
where the time goes:
time: 480 us; the launch traced here: 473 us
  blocking collectives  125 us (26%)
  waiting for transfers between devices  122 us (25%)
  local copies, waits for them, and re-layouts  90.3 us (19%)
  matrix products  63.8 us (13%)
  starting transfers between devices  29.9 us (6%)
  other arithmetic  26.1 us (5%)
  between operations  14.3 us (3%)
    all_gather x1, blocking collectives, body(): col_done = lax.all_gather(far_local, 'col', axis=1, tiled=True)  125 us
    all_gather x1, waiting for transfers between devices, body(): far_keys = lax.all_gather(col_done, 'row', axis=1, tiled=True)  106 us
    slice x16, local copies, waits for them, and re-layouts, pair_step(): valtan_parts.append(columns(block[3]).reshape(count, 2, head_dim))  30.8 us
    unnamed x25, local copies, waits for them, and re-layouts  23.5 us
    ppermute x2, starting transfers between devices, with_halo(): lax.ppermute(head, axis, [((i + 1) % count, i) for i in range(ends)])  20.5 us
    dot_general x24, matrix products, pair_step(): jnp.einsum('qhd,khd->hqk', query_pair, keytan_part, preferred_element_typ...  14.7 us
    concatenate x2, other arithmetic, with_halo(): jnp.concatenate([lax.ppermute(tail, axis, [(i, (i + 1) % count) for i in...  12.6 us
    dynamic_slice x112, local copies, waits for them, and re-layouts, columns(): return lax.dynamic_slice_in_dim(array, start, pair_width, array.ndim - 1)  11.6 us
  transfers between devices with their start and end apart: 7, of which 4 were waited for; matrix products, arithmetic and copies ran while one was open for 8% of the time, Pallas kernels for 0%

commit v1 on v0

v1 whole, which is shorter than its diff:
```python
import functools
import math

import jax
import jax.numpy as jnp
import numpy as np
from jax import lax
from jax.experimental import pallas as pl
from jax.experimental.pallas import tpu as pltpu
from jax.sharding import PartitionSpec as P

HEADS = 16
HEAD_DIM = 72
D = 1152
WIN = 16
CELLS = WIN * WIN
NX, NY, NZ = 4, 4, 16
LANES = 384
CHUNKS = D // LANES
MESH = pl.DeviceIdType.MESH
LOG2E = math.log2(math.e)
SCALE = HEAD_DIM**-0.5
NEG = -1e30

OWN, TOP, BOTTOM, LEFT, RIGHT = 0, 32, 48, 64, 80
TL, TR, BL, BR = 96, 104, 112, 120
NEAR, FAR, PAD = 128, 136, 200
GROUPS = 208
KEYS = GROUPS * 8
BLOCK = 32


def prep_kernel(w_ref, k_ref, v_ref, kt_ref, vt_ref, stack_ref, near_ref, far_ref):
    w = w_ref[...]
    hi = w.astype(jnp.bfloat16)
    rest = w - hi.astype(jnp.float32)
    mid = rest.astype(jnp.bfloat16)
    low = (rest - mid.astype(jnp.float32)).astype(jnp.bfloat16)
    far_rows = []
    for f, ref in enumerate((k_ref, v_ref, kt_ref, vt_ref)):
        cells = ref[...]
        stack_ref[f] = cells
        flat = cells.reshape(CELLS, D)
        pooled = jnp.dot(low, flat, preferred_element_type=jnp.float32)
        pooled += jnp.dot(mid, flat, preferred_element_type=jnp.float32)
        pooled += jnp.dot(hi, flat, preferred_element_type=jnp.float32)
        near_ref[f] = pooled[:16].astype(jnp.bfloat16)
        far_rows.append(pooled[16:17])
    far_ref[...] = jnp.concatenate(far_rows, axis=0).astype(jnp.bfloat16)


def place():
    r, c = lax.axis_index("row"), lax.axis_index("col")
    y, x = r // 8, lax.rem(r, 4)
    z = lax.rem(r // 4, 2) * 8 + c // 2
    return r, c, x, y, z, lax.rem(c, 2)


def device(x, y, z, core):
    return (y * 8 + (z // 8) * 4 + x, lax.rem(z, 8) * 2 + core)


def main_kernel(
    stack, near_in, far_in, q_in, qt_in, bias_ref,
    mix_ref, tan_ref,
    keys, zbuf, q_ref, qt_ref, s_ref, t_ref, w_ref, mix_acc, tan_acc,
    halo_send, halo_recv, misc_send, misc_recv, local_sem,
):
    r, c, x, y, z, core = place()
    up, down, west, east = r > 0, r < 31, c > 0, c < 15
    z_peers = [lax.rem(z + k, NZ) for k in range(1, NZ)]
    x_peers = [lax.rem(x + k, NX) for k in range(1, NX)]
    y_peers = [lax.rem(y + k, NY) for k in range(1, NY)]
    x_near = x + 1 - 2 * lax.rem(x, 2)
    near_peers = [device(x_near, y, z, core), device(x, y, z, 1 - core), device(x_near, y, z, 1 - core)]

    def lanes(chunk):
        return pl.ds(pl.multiple_of(chunk * LANES, 128), LANES)

    def part(first, count, chunk=None):
        width = slice(None) if chunk is None else lanes(chunk)
        return keys.at[:, pl.ds(first, count), :, width]

    def strips(chunk):
        out = []
        for half in range(2):
            out.append((down, stack.at[:, pl.ds(8, 8), half, :, lanes(chunk)], TOP + 8 * half, 8, (r + 1, c), up))
            out.append((up, stack.at[:, pl.ds(0, 8), half, :, lanes(chunk)], BOTTOM + 8 * half, 8, (r - 1, c), down))
        return out

    def sides(chunk):
        return [
            (east, stack.at[:, :, 1, :, lanes(chunk)], LEFT, 16, (r, c + 1), west),
            (west, stack.at[:, :, 0, :, lanes(chunk)], RIGHT, 16, (r, c - 1), east),
        ]

    def corners(chunk):
        return [
            (up & east, part(TOP + 8, 8, chunk), TL, 8, (r, c + 1), up & west),
            (up & west, part(TOP, 8, chunk), TR, 8, (r, c - 1), up & east),
            (down & east, part(BOTTOM + 8, 8, chunk), BL, 8, (r, c + 1), down & west),
            (down & west, part(BOTTOM, 8, chunk), BR, 8, (r, c - 1), down & east),
        ]

    def run(make, base, chunk, what):
        for n, (sends, src, first, count, target, receives) in enumerate(make(chunk)):
            slot = chunk * 10 + base + n
            copy = pltpu.make_async_remote_copy(
                src_ref=src, dst_ref=part(first, count, chunk),
                send_sem=halo_send.at[slot], recv_sem=halo_recv.at[slot],
                device_id=target, device_id_type=MESH,
            )
            if what == "start":
                pl.when(sends)(copy.start)
            elif what == "recv":
                pl.when(receives)(copy.wait_recv)
            else:
                pl.when(sends)(copy.wait_send)

    def to(src, dst, slot, target):
        return pltpu.make_async_remote_copy(
            src_ref=src, dst_ref=dst, send_sem=misc_send.at[slot], recv_sem=misc_recv.at[slot],
            device_id=target, device_id_type=MESH,
        )

    def drained(ref, sem):
        pltpu.make_async_copy(ref, ref, sem).wait()

    local = [
        pltpu.make_async_copy(stack.at[:, :, half], keys.at[:, pl.ds(OWN + 16 * half, 16)], local_sem.at[half])
        for half in range(2)
    ]
    near_slot = NEAR + 2 * (lax.rem(x, 2) * 2 + core)
    local.append(pltpu.make_async_copy(near_in, part(near_slot, 2), local_sem.at[2]))
    local.append(pltpu.make_async_copy(q_in, q_ref, local_sem.at[3]))
    local.append(pltpu.make_async_copy(qt_in, qt_ref, local_sem.at[4]))
    for copy in local:
        copy.start()

    barrier = pltpu.get_barrier_semaphore()

    def greet(target):
        pl.semaphore_signal(barrier, inc=1, device_id=target, device_id_type=MESH)

    for cond, target in ((down, (r + 1, c)), (up, (r - 1, c)), (east, (r, c + 1)), (west, (r, c - 1))):
        pl.when(cond)(functools.partial(greet, target))
    fixed = (
        [device(x, y, p, core) for p in z_peers]
        + [device(p, y, z, core) for p in x_peers]
        + [device(x, p, z, core) for p in y_peers]
        + [device(x, y, z, 1 - core), device(x_near, y, z, 1 - core)]
    )
    for target in fixed:
        greet(target)
    edges = sum(cond.astype(jnp.int32) for cond in (down, up, east, west))
    pl.semaphore_wait(barrier, len(fixed) + edges)

    for p in z_peers:
        to(far_in, zbuf.at[z], 0, device(x, y, p, core)).start()
    own_far = pltpu.make_async_copy(far_in, zbuf.at[z], local_sem.at[5])
    own_far.start()
    for target in near_peers:
        to(near_in, part(near_slot, 2), 4, target).start()
    for chunk in range(CHUNKS):
        run(strips, 0, chunk, "start")
        run(sides, 4, chunk, "start")

    def clear(first, count):
        keys[:, pl.ds(first, count)] = jnp.zeros((4, count, 8, D), jnp.bfloat16)

    clear(PAD, GROUPS - PAD)
    for present, first, count in ((up, TOP, 16), (down, BOTTOM, 16), (west, LEFT, 16), (east, RIGHT, 16)):
        pl.when(jnp.logical_not(present))(functools.partial(clear, first, count))
    for present, first in ((up & west, TL), (up & east, TR), (down & west, BL), (down & east, BR)):
        pl.when(jnp.logical_not(present))(functools.partial(clear, first, 8))

    far_group = FAR + 32 * core + 8 * y + 2 * x
    own_far.wait()
    drained(zbuf.at[pl.ds(0, NZ - 1)], misc_recv.at[0])
    for f in range(4):
        cells = jnp.concatenate([zbuf[n].astype(jnp.float32)[f : f + 1] for n in range(NZ)], axis=0)
        keys[f, pl.ds(far_group, 2)] = cells.astype(jnp.bfloat16).reshape(2, 8, D)
    for copy in local:
        copy.wait()
    for p in x_peers:
        to(part(far_group, 2), part(far_group, 2), 1, device(p, y, z, core)).start()
    drained(part(FAR, 6), misc_recv.at[1])
    far_y = FAR + 32 * core + 8 * y
    for p in y_peers:
        to(part(far_y, 8), part(far_y, 8), 2, device(x, p, z, core)).start()
    run(strips, 0, 0, "recv")
    run(corners, 6, 0, "start")
    drained(part(FAR, 24), misc_recv.at[2])
    far_core = FAR + 32 * core
    swap = to(part(far_core, 32), part(far_core, 32), 3, device(x, y, z, 1 - core))
    swap.start()
    drained(part(NEAR, 6), misc_recv.at[4])

    def load(f, tile, count):
        width = 128 * count
        return keys[f, :, :, pl.ds(pl.multiple_of(tile * 128, 128), width)].reshape(KEYS, width)

    def query(ref, tile, count):
        width = 128 * count
        return ref[:, :, pl.ds(pl.multiple_of(tile * 128, 128), width)].reshape(CELLS, width)

    def in_head(head, tile, count):
        lane = lax.broadcasted_iota(jnp.int32, (1, 128 * count), 1) + tile * 128 - head * HEAD_DIM
        return (lane >= 0) & (lane < HEAD_DIM)

    def nt(a, b):
        return lax.dot_general(a, b, (((1,), (1,)), ((), ())), preferred_element_type=jnp.float32)

    def nn(a, b):
        return jnp.dot(a, b, preferred_element_type=jnp.float32)

    def softmax(head):
        bias = bias_ref[head]

        def block(n, carry):
            rows = pl.ds(pl.multiple_of(n * BLOCK, BLOCK), BLOCK)
            top = None
            for tile in range(KEYS // 128):
                cols = slice(tile * 128, tile * 128 + 128)
                scores = s_ref[rows, cols] * (SCALE * LOG2E) + bias[:, cols]
                s_ref[rows, cols] = scores
                top = scores if top is None else jnp.maximum(top, scores)
            top = jnp.max(top, axis=1, keepdims=True)
            total = None
            for tile in range(KEYS // 128):
                cols = slice(tile * 128, tile * 128 + 128)
                expd = jnp.exp2(s_ref[rows, cols] - top)
                s_ref[rows, cols] = expd
                total = expd if total is None else total + expd
            inverse = 1.0 / jnp.sum(total, axis=1, keepdims=True)
            late = pl.ds(pl.multiple_of(CELLS + n * BLOCK, BLOCK), BLOCK)
            row_total = None
            for tile in range(KEYS // 128):
                cols = slice(tile * 128, tile * 128 + 128)
                weights = s_ref[rows, cols] * inverse
                product = weights * (t_ref[rows, cols] * SCALE)
                w_ref[rows, cols] = weights.astype(jnp.bfloat16)
                w_ref[late, cols] = product.astype(jnp.bfloat16)
                row_total = product if row_total is None else row_total + product
            row_sum = jnp.sum(row_total, axis=1, keepdims=True)
            t_ref[rows, 0:128] = jnp.broadcast_to(row_sum, (BLOCK, 128))
            return carry

        lax.fori_loop(0, CELLS // BLOCK, block, 0)

    def finish(head, tile, count, mix, product_mix, weight_tan):
        cols = pl.ds(pl.multiple_of(tile * 128, 128), 128 * count)
        keep = in_head(head, tile, count)
        row_total = t_ref[:, 0:128]
        if count == 2:
            row_total = jnp.concatenate([row_total, row_total], axis=1)
        mix_tan = product_mix + weight_tan - row_total * mix
        mix_acc[:, cols] = jnp.where(keep, mix, mix_acc[:, cols])
        tan_acc[:, cols] = jnp.where(keep, mix_tan, tan_acc[:, cols])

    def step(n, carry):
        late = (n >= 4).astype(jnp.int32)
        head, tile = 2 * n + late, n + late
        mask = in_head(head, tile, 1).astype(jnp.float32).astype(jnp.bfloat16)
        q = query(q_ref, tile, 1) * mask
        qt = query(qt_ref, tile, 1) * mask
        both = jnp.concatenate([jnp.concatenate([q, jnp.zeros_like(q)], 1), jnp.concatenate([qt, q], 1)], 0)
        scores = nt(both, jnp.concatenate([load(0, tile, 1), load(2, tile, 1)], 1))
        s_ref[...] = scores[:CELLS]
        t_ref[...] = scores[CELLS:]
        softmax(head)
        mixed = nn(w_ref[...], jnp.concatenate([load(1, tile, 1), load(3, tile, 1)], 1))
        finish(head, tile, 1, mixed[:CELLS, :128], mixed[CELLS:, :128], mixed[:CELLS, 128:])
        head, tile = 2 * n + 1 - late, n
        mask = in_head(head, tile, 2).astype(jnp.float32).astype(jnp.bfloat16)
        q = query(q_ref, tile, 2) * mask
        qt = query(qt_ref, tile, 2) * mask
        scores = nt(jnp.concatenate([q, qt], 0), load(0, tile, 2))
        s_ref[...] = scores[:CELLS]
        t_ref[...] = scores[CELLS:] + nt(q, load(2, tile, 2))
        softmax(head)
        mixed = nn(w_ref[...], load(1, tile, 2))
        finish(head, tile, 2, mixed[:CELLS], mixed[CELLS:], nn(w_ref[pl.ds(0, CELLS), :], load(3, tile, 2)))
        return carry

    def chunk_step(chunk, carry):
        @pl.when(chunk > 0)
        def _():
            run(strips, 0, chunk, "recv")
            run(corners, 6, chunk, "start")

        @pl.when(chunk == 0)
        def _():
            swap.wait_recv()

        run(sides, 4, chunk, "recv")
        run(corners, 6, chunk, "recv")
        lax.fori_loop(jnp.maximum(3 * chunk - 1, 0), 3 * chunk + 2, step, 0)
        return carry

    lax.fori_loop(0, CHUNKS, chunk_step, 0)
    mix_ref[...] = mix_acc[...].astype(jnp.bfloat16).reshape(WIN, WIN, D)
    tan_ref[...] = tan_acc[...].astype(jnp.bfloat16).reshape(WIN, WIN, D)

    for chunk in range(CHUNKS):
        run(strips, 0, chunk, "sent")
        run(sides, 4, chunk, "sent")
        run(corners, 6, chunk, "sent")
    drained(zbuf.at[pl.ds(0, NZ - 1)], misc_send.at[0])
    drained(part(FAR, 6), misc_send.at[1])
    drained(part(FAR, 24), misc_send.at[2])
    swap.wait_send()
    drained(part(NEAR, 6), misc_send.at[4])


def pool_weights(pool_near, pool_far):
    cell = np.arange(CELLS)
    block = (cell // 64) * 4 + (cell % 16) // 4
    member = jnp.asarray(np.arange(16)[:, None] == block[None, :])
    near = jnp.where(member, jnp.tile(pool_near, (4, 4)).reshape(1, CELLS), 0.0)
    return jnp.concatenate([near, pool_far.reshape(1, CELLS), jnp.zeros((7, CELLS), jnp.float32)], axis=0)


def key_bias(level_bias):
    r, c = lax.axis_index("row"), lax.axis_index("col")
    group = np.arange(GROUPS)

    def within(first, count):
        return (group >= first) & (group < first + count)

    top = within(TOP, 16) | within(TL, 8) | within(TR, 8)
    bottom = within(BOTTOM, 16) | within(BL, 8) | within(BR, 8)
    left = within(LEFT, 16) | within(TL, 8) | within(BL, 8)
    right = within(RIGHT, 16) | within(TR, 8) | within(BR, 8)
    gone = (r == 0) & top | (r == 31) & bottom | (c == 0) & left | (c == 15) & right
    gone = gone | (group >= PAD)
    bias = jnp.where(within(NEAR, 8), level_bias[0][:, None], jnp.where(within(FAR, 64), level_bias[1][:, None], 0.0))
    bias = jnp.where(gone[None, :], NEG, bias * LOG2E)
    return jnp.repeat(bias, 8, axis=1).reshape(HEADS, 1, KEYS)


def body(query_field, key_field, value_field, query_tan, key_tan, value_tan, pool_near, pool_far, level_bias):
    vmem = pl.BlockSpec(memory_space=pltpu.VMEM)
    anywhere = pl.BlockSpec(memory_space=pl.ANY)
    field = jax.ShapeDtypeStruct((WIN, WIN, D), jnp.bfloat16)
    stack, near, far = pl.pallas_call(
        prep_kernel,
        out_shape=(
            jax.ShapeDtypeStruct((4, WIN, WIN, D), jnp.bfloat16),
            jax.ShapeDtypeStruct((4, 16, D), jnp.bfloat16),
            jax.ShapeDtypeStruct((4, D), jnp.bfloat16),
        ),
        in_specs=[vmem] * 5,
        out_specs=(vmem, vmem, vmem),
        name="prep",
    )(pool_weights(pool_near, pool_far), key_field, value_field, key_tan, value_tan)
    halo = 10 * CHUNKS
    return pl.pallas_call(
        main_kernel,
        out_shape=(field, field),
        in_specs=[anywhere] * 5 + [vmem],
        out_specs=(vmem, vmem),
        scratch_shapes=[
            pltpu.VMEM((4, GROUPS, 8, D), jnp.bfloat16),
            pltpu.VMEM((NZ, 4, D), jnp.bfloat16),
            pltpu.VMEM((WIN, WIN, D), jnp.bfloat16),
            pltpu.VMEM((WIN, WIN, D), jnp.bfloat16),
            pltpu.VMEM((CELLS, KEYS), jnp.float32),
            pltpu.VMEM((CELLS, KEYS), jnp.float32),
            pltpu.VMEM((2 * CELLS, KEYS), jnp.bfloat16),
            pltpu.VMEM((CELLS, D), jnp.float32),
            pltpu.VMEM((CELLS, D), jnp.float32),
            pltpu.SemaphoreType.DMA((halo,)),
            pltpu.SemaphoreType.DMA((halo,)),
            pltpu.SemaphoreType.DMA((5,)),
            pltpu.SemaphoreType.DMA((5,)),
            pltpu.SemaphoreType.DMA((6,)),
        ],
        compiler_params=pltpu.CompilerParams(
            collective_id=0, has_side_effects=True, vmem_limit_bytes=60 * 1024 * 1024
        ),
        name="focal",
    )(
        stack.reshape(4, WIN, 2, 8, D), near.reshape(4, 2, 8, D), far, query_field, query_tan, key_bias(level_bias)
    )


def solution(mesh):
    spec = P("row", "col", None)
    return jax.shard_map(
        body, mesh=mesh, in_specs=(spec,) * 6 + (P(),) * 3, out_specs=(spec, spec), check_vma=False
    )
```

time: 480 us -> 249 us (0.52); the launches traced: 473 us -> 248 us
  Pallas kernels: 0 us -> 237 us
  blocking collectives: 125 us -> 0 us
  waiting for transfers between devices: 122 us -> 0 us
  local copies, waits for them, and re-layouts: 90.3 us -> 7.23 us
  matrix products: 63.8 us -> 0 us
  starting transfers between devices: 29.9 us -> 0 us
  other arithmetic: 26.1 us -> 2.93 us
  between operations: 14.3 us -> 0.67 us
    pallas_call x0 -> x2, Pallas kernels: none -> 237 us  [the longest x1 234 us: body(): pl.pallas_call(main_kernel, out_shape=(field, field), in_specs=[anywhere]...]
    all_gather x1 -> x0, blocking collectives: 125 us -> none  [body(): col_done = lax.all_gather(far_local, 'col', axis=1, tiled=True)]
    all_gather x1 -> x0, waiting for transfers between devices: 106 us -> none  [body(): far_keys = lax.all_gather(col_done, 'row', axis=1, tiled=True)]
    dot_general x146 -> x0, matrix products: 63.8 us -> none  [the longest x24 14.7 us: pair_step(): jnp.einsum('qhd,khd->hqk', query_pair, keytan_part, preferred_element_typ...]
    slice x26 -> x0, local copies, waits for them, and re-layouts: 35.5 us -> none  [the longest x16 30.8 us: pair_step(): valtan_parts.append(columns(block[3]).reshape(count, 2, head_dim))]
    ppermute x6 -> x0, starting transfers between devices: 29.8 us -> none  [the longest x2 20.5 us: with_halo(): lax.ppermute(head, axis, [((i + 1) % count, i) for i in range(ends)])]
    unnamed x25 -> x2, local copies, waits for them, and re-layouts: 23.5 us -> 3.85 us
    ppermute x6 -> x0, waiting for transfers between devices: 16.1 us -> none  [the longest x2 5.85 us: partner(): return lax.ppermute(block, axis, route)]
  transfers between devices with their start and end apart: 7 -> 0, of which waited for: 4 -> 0; matrix products, arithmetic and copies ran while one was open for 8% -> 0% of each run, Pallas kernels for 0% -> 0%
where the time goes in v1:
time: 249 us; the launch traced here: 248 us
  Pallas kernels  237 us (95%)
  local copies, waits for them, and re-layouts  7.23 us (3%)
  other arithmetic  2.93 us (1%)
    pallas_call x1, Pallas kernels, body(): pl.pallas_call(main_kernel, out_shape=(field, field), in_specs=[anywhere]...  234 us

profile of v1, /device:TPU:25, one launch (start us, length us, event | category | flops | bytes accessed | tf_op | source)
XLA Modules:
  0.0 248.3 jit_solution(14778601773977768133)
XLA Ops:
  0.6 0.7 or_or_fusion
  1.4 0.1 pad.2.clone
  1.5 0.8 reshape.18
  2.2 0.8 slice_bitcast_fusion.1
  3.0 0.7 tile.2
  3.7 0.1 broadcast_in_dim.65
  3.8 0.7 broadcast_select_fusion
  4.5 0.7 maximum_maximum_fusion.w_ref
  5.2 0.8 multiply_select_fusion
  6.0 0.1 broadcast_bitcast_fusion
  6.1 0.9 copy.19.bias_ref
  7.0 3.9 %prep.1 = (bf16[4,16,16,1152]{3,2,1,0:T(8,128)(2,1)}, bf16[4,16,1152]{2,1,0:T(8,128)(2,1)}, bf16[4,1152]{1,0:T(4,128)(2,1)}) custom-call(f32[24,256]{1,0:T(8,128)} %maximum_maximum_fusion.w_ref, bf16[16,16,1152]{2,1,0:T(8,128)(2,1)} %k_ref.1, bf16[16,16,1152]{2,1,0:T(8,128)(2,1)} %v_ref.1, bf16[16,16,1152]{2,1,0:T(8,128)(2,1)} %kt_ref.1, ...), custom_call_target="tpu_custom_call" | custom-call | tf_op jit(solution)/shard_map/prep/pallas_call | solution.py:346
  10.9 233.5 %focal.1 = (bf16[16,16,1152]{2,1,0:T(8,128)(2,1)}, bf16[16,16,1152]{2,1,0:T(8,128)(2,1)}) custom-call(bf16[4,16,2,8,1152]{4,3,2,1,0:T(8,128)(2,1)} %bitcast.8, bf16[4,2,8,1152]{3,2,1,0:T(8,128)(2,1)} %bitcast.9, bf16[4,1152]{1,0:T(4,128)(2,1)} %get-tuple-element.7.far_in, bf16[16,16,1152]{2,1,0:T(8,128)(2,1)} %q_in.1, bf16[16,16,1152]{2,1,0:T(8,128)(2,1)} %qt_in.1, ...), custom_call_target="tpu_custom_call" | custom-call | tf_op jit(solution)/shard_map/focal/pallas_call | solution.py:358
  244.4 1.9 copy.22
  246.3 1.9 copy.23
  (1 shorter events, 0.0 us)

commit v2 on v1

--- a/solution.py
+++ b/solution.py
@@ -15,8 +15,8 @@
 WIN = 16
 CELLS = WIN * WIN
 NX, NY, NZ = 4, 4, 16
-LANES = 384
-CHUNKS = D // LANES
+EDGES = (0, 384, 640, 896, 1152)
+CHUNKS = len(EDGES) - 1
 MESH = pl.DeviceIdType.MESH
 LOG2E = math.log2(math.e)
 SCALE = HEAD_DIM**-0.5
@@ -24,7 +24,7 @@
 
 OWN, TOP, BOTTOM, LEFT, RIGHT = 0, 32, 48, 64, 80
 TL, TR, BL, BR = 96, 104, 112, 120
-NEAR, FAR, PAD = 128, 136, 200
+NEAR, PAD, FAR = 128, 136, 144
 GROUPS = 208
 KEYS = GROUPS * 8
 BLOCK = 32
@@ -63,8 +63,8 @@
 def main_kernel(
     stack, near_in, far_in, q_in, qt_in, bias_ref,
     mix_ref, tan_ref,
-    keys, zbuf, q_ref, qt_ref, s_ref, t_ref, w_ref, mix_acc, tan_acc,
-    halo_send, halo_recv, misc_send, misc_recv, local_sem,
+    keys, zbuf, relay, q_ref, qt_ref, s_ref, t_ref, w_ref, mix_acc, tan_acc,
+    halo_send, halo_recv, relay_send, relay_recv, misc_send, misc_recv, local_sem,
 ):
     r, c, x, y, z, core = place()
     up, down, west, east = r > 0, r < 31, c > 0, c < 15
@@ -74,19 +74,55 @@
     x_near = x + 1 - 2 * lax.rem(x, 2)
     near_peers = [device(x_near, y, z, core), device(x, y, z, 1 - core), device(x_near, y, z, 1 - core)]
 
-    def lanes(chunk):
-        return pl.ds(pl.multiple_of(chunk * LANES, 128), LANES)
-
-    def part(first, count, chunk=None):
-        width = slice(None) if chunk is None else lanes(chunk)
+    def lanes(chunk, last=None):
+        last = chunk if last is None else last
+        return pl.ds(EDGES[chunk], EDGES[last + 1] - EDGES[chunk])
+
+    def part(first, count, chunk=None, last=None):
+        width = slice(None) if chunk is None else lanes(chunk, last)
         return keys.at[:, pl.ds(first, count), :, width]
 
+    place_x = lax.rem(r, 4)
+    far_down, far_up = down & (place_x == 3), up & (place_x == 0)
+    hops = jnp.where(place_x >= 2, 2, -2)
+    paired = (r + hops >= 0) & (r + hops < 32)
+    relays_down, relays_up = paired & (place_x == 2), paired & (place_x == 1)
+
     def strips(chunk):
-        out = []
-        for half in range(2):
-            out.append((down, stack.at[:, pl.ds(8, 8), half, :, lanes(chunk)], TOP + 8 * half, 8, (r + 1, c), up))
-            out.append((up, stack.at[:, pl.ds(0, 8), half, :, lanes(chunk)], BOTTOM + 8 * half, 8, (r - 1, c), down))
-        return out
+        low = [stack.at[:, pl.ds(8, 8), half, :, lanes(chunk)] for half in range(2)]
+        high = [stack.at[:, pl.ds(0, 8), half, :, lanes(chunk)] for half in range(2)]
+        return [
+            (down, low[0], TOP, 8, (r + 1, c), up),
+            (up, high[0], BOTTOM, 8, (r - 1, c), down),
+            (down & (place_x != 3), low[1], TOP + 8, 8, (r + 1, c), up),
+            (up & (place_x != 0), high[1], BOTTOM + 8, 8, (r - 1, c), down),
+        ]
+
+    def relay_in(chunk, what):
+        for n, cond, row, target in ((2, far_down, 8, (r - 1, c)), (3, far_up, 0, (r + 1, c))):
+            copy = pltpu.make_async_remote_copy(
+                src_ref=stack.at[:, pl.ds(row, 8), 1, :, lanes(chunk)], dst_ref=relay.at[:, :, :, lanes(chunk)],
+                send_sem=halo_send.at[chunk * 10 + n], recv_sem=relay_recv.at[chunk],
+                device_id=target, device_id_type=MESH,
+            )
+            pl.when(cond)(copy.start if what == "start" else copy.wait_send)
+
+    def relay_out(chunk, what):
+        for n, cond, first, row in ((2, relays_down, TOP + 8, r + 2), (3, relays_up, BOTTOM + 8, r - 2)):
+            copy = pltpu.make_async_remote_copy(
+                src_ref=relay.at[:, :, :, lanes(chunk)], dst_ref=part(first, 8, chunk),
+                send_sem=relay_send.at[chunk], recv_sem=halo_recv.at[chunk * 10 + n],
+                device_id=(row, c), device_id_type=MESH,
+            )
+            if what == "start":
+                arrived = relay.at[:, :, :, lanes(chunk)]
+
+                @pl.when(cond)
+                def _(copy=copy, arrived=arrived):
+                    drained(arrived, relay_recv.at[chunk])
+                    copy.start()
+            else:
+                pl.when(cond)(copy.wait_send)
 
     def sides(chunk):
         return [
@@ -152,28 +188,30 @@
     )
     for target in fixed:
         greet(target)
-    edges = sum(cond.astype(jnp.int32) for cond in (down, up, east, west))
+    pl.when(paired)(functools.partial(greet, (r + hops, c)))
+    edges = sum(cond.astype(jnp.int32) for cond in (down, up, east, west, paired))
     pl.semaphore_wait(barrier, len(fixed) + edges)
 
+    relay_in(0, "start")
     for p in z_peers:
         to(far_in, zbuf.at[z], 0, device(x, y, p, core)).start()
     own_far = pltpu.make_async_copy(far_in, zbuf.at[z], local_sem.at[5])
     own_far.start()
+    run(strips, 0, 0, "start")
+    run(sides, 4, 0, "start")
     for target in near_peers:
         to(near_in, part(near_slot, 2), 4, target).start()
-    for chunk in range(CHUNKS):
-        run(strips, 0, chunk, "start")
-        run(sides, 4, chunk, "start")
 
     def clear(first, count):
         keys[:, pl.ds(first, count)] = jnp.zeros((4, count, 8, D), jnp.bfloat16)
 
-    clear(PAD, GROUPS - PAD)
+    clear(PAD, FAR - PAD)
     for present, first, count in ((up, TOP, 16), (down, BOTTOM, 16), (west, LEFT, 16), (east, RIGHT, 16)):
         pl.when(jnp.logical_not(present))(functools.partial(clear, first, count))
     for present, first in ((up & west, TL), (up & east, TR), (down & west, BL), (down & east, BR)):
         pl.when(jnp.logical_not(present))(functools.partial(clear, first, 8))
 
+    relay_out(0, "start")
     far_group = FAR + 32 * core + 8 * y + 2 * x
     own_far.wait()
     drained(zbuf.at[pl.ds(0, NZ - 1)], misc_recv.at[0])
@@ -184,16 +222,36 @@
         copy.wait()
     for p in x_peers:
         to(part(far_group, 2), part(far_group, 2), 1, device(p, y, z, core)).start()
+    for chunk in range(1, CHUNKS):
+        relay_in(chunk, "start")
     drained(part(FAR, 6), misc_recv.at[1])
-    far_y = FAR + 32 * core + 8 * y
-    for p in y_peers:
-        to(part(far_y, 8), part(far_y, 8), 2, device(x, p, z, core)).start()
-    run(strips, 0, 0, "recv")
-    run(corners, 6, 0, "start")
-    drained(part(FAR, 24), misc_recv.at[2])
-    far_core = FAR + 32 * core
-    swap = to(part(far_core, 32), part(far_core, 32), 3, device(x, y, z, 1 - core))
-    swap.start()
+    far_y, far_core = FAR + 32 * core + 8 * y, FAR + 32 * core
+    groups = ((0, 0), (1, CHUNKS - 1))
+
+    def send_y(n):
+        for p in y_peers:
+            to(part(far_y, 8, *groups[n]), part(far_y, 8, *groups[n]), 2 + n, device(x, p, z, core)).start()
+
+    swaps = [
+        to(part(far_core, 32, *span), part(far_core, 32, *span), 5 + n, device(x, y, z, 1 - core))
+        for n, span in enumerate(groups)
+    ]
+    send_y(0)
+    drained(part(FAR, 24, *groups[0]), misc_recv.at[2])
+    swaps[0].start()
+    send_y(1)
+
+    def advance(chunk):
+        run(strips, 0, chunk, "recv")
+        run(corners, 6, chunk, "start")
+        if chunk + 1 < CHUNKS:
+            run(strips, 0, chunk + 1, "start")
+            run(sides, 4, chunk + 1, "start")
+            relay_out(chunk + 1, "start")
+
+    advance(0)
+    drained(part(FAR, 24, *groups[1]), misc_recv.at[3])
+    swaps[1].start()
     drained(part(NEAR, 6), misc_recv.at[4])
 
     def load(f, tile, count):
@@ -283,20 +341,19 @@
         finish(head, tile, 2, mixed[:CELLS], mixed[CELLS:], nn(w_ref[pl.ds(0, CELLS), :], load(3, tile, 2)))
         return carry
 
-    def chunk_step(chunk, carry):
-        @pl.when(chunk > 0)
-        def _():
-            run(strips, 0, chunk, "recv")
-            run(corners, 6, chunk, "start")
-
-        @pl.when(chunk == 0)
-        def _():
-            swap.wait_recv()
-
-        run(sides, 4, chunk, "recv")
-        run(corners, 6, chunk, "recv")
-        lax.fori_loop(jnp.maximum(3 * chunk - 1, 0), 3 * chunk + 2, step, 0)
-        return carry
+    def chunk_step(n, carry):
+        for chunk in range(CHUNKS):
+
+            @pl.when(n == chunk)
+            def _(chunk=chunk):
+                if chunk:
+                    advance(chunk)
+                if chunk < 2:
+                    swaps[chunk].wait_recv()
+                run(sides, 4, chunk, "recv")
+                run(corners, 6, chunk, "recv")
+
+        return lax.fori_loop(2 * n, 2 * n + 2, step, carry)
 
     lax.fori_loop(0, CHUNKS, chunk_step, 0)
     mix_ref[...] = mix_acc[...].astype(jnp.bfloat16).reshape(WIN, WIN, D)
@@ -306,10 +363,13 @@
         run(strips, 0, chunk, "sent")
         run(sides, 4, chunk, "sent")
         run(corners, 6, chunk, "sent")
+        relay_in(chunk, "sent")
+        relay_out(chunk, "sent")
     drained(zbuf.at[pl.ds(0, NZ - 1)], misc_send.at[0])
     drained(part(FAR, 6), misc_send.at[1])
-    drained(part(FAR, 24), misc_send.at[2])
-    swap.wait_send()
+    for n, span in enumerate(groups):
+        drained(part(FAR, 24, *span), misc_send.at[2 + n])
+        swaps[n].wait_send()
     drained(part(NEAR, 6), misc_send.at[4])
 
 
@@ -333,7 +393,7 @@
     left = within(LEFT, 16) | within(TL, 8) | within(BL, 8)
     right = within(RIGHT, 16) | within(TR, 8) | within(BR, 8)
     gone = (r == 0) & top | (r == 31) & bottom | (c == 0) & left | (c == 15) & right
-    gone = gone | (group >= PAD)
+    gone = gone | within(PAD, 8)
     bias = jnp.where(within(NEAR, 8), level_bias[0][:, None], jnp.where(within(FAR, 64), level_bias[1][:, None], 0.0))
     bias = jnp.where(gone[None, :], NEG, bias * LOG2E)
     return jnp.repeat(bias, 8, axis=1).reshape(HEADS, 1, KEYS)
@@ -363,6 +423,7 @@
         scratch_shapes=[
             pltpu.VMEM((4, GROUPS, 8, D), jnp.bfloat16),
             pltpu.VMEM((NZ, 4, D), jnp.bfloat16),
+            pltpu.VMEM((4, 8, 8, D), jnp.bfloat16),
             pltpu.VMEM((WIN, WIN, D), jnp.bfloat16),
             pltpu.VMEM((WIN, WIN, D), jnp.bfloat16),
             pltpu.VMEM((CELLS, KEYS), jnp.float32),
@@ -372,8 +433,10 @@
             pltpu.VMEM((CELLS, D), jnp.float32),
             pltpu.SemaphoreType.DMA((halo,)),
             pltpu.SemaphoreType.DMA((halo,)),
-            pltpu.SemaphoreType.DMA((5,)),
-            pltpu.SemaphoreType.DMA((5,)),
+            pltpu.SemaphoreType.DMA((CHUNKS,)),
+            pltpu.SemaphoreType.DMA((CHUNKS,)),
+            pltpu.SemaphoreType.DMA((7,)),
+            pltpu.SemaphoreType.DMA((7,)),
             pltpu.SemaphoreType.DMA((6,)),
         ],
         compiler_params=pltpu.CompilerParams(

time: 249 us -> 196 us (0.79)
  the two profiles are of different devices: /device:TPU:25 before, /device:TPU:68 now
where the time goes in v2:
time: 196 us
  Pallas kernels  185 us (94%)
  local copies, waits for them, and re-layouts  7.23 us (4%)
  other arithmetic  2.93 us (1%)
    pallas_call x1, Pallas kernels, body(): pl.pallas_call(main_kernel, out_shape=(field, field), in_specs=[anywhere]...  181 us

profile of v2, /device:TPU:68, one launch (start us, length us, event | category | flops | bytes accessed | tf_op | source)
XLA Modules:
  0.0 195.6 jit_solution(13980491986370841019)
XLA Ops:
  0.6 0.7 or_or_fusion
  1.4 0.1 pad.2.clone
  1.5 0.8 reshape.18
  2.2 0.8 slice_bitcast_fusion.1
  3.0 0.7 tile.2
  3.7 0.1 broadcast_in_dim.65
  3.8 0.7 broadcast_select_fusion
  4.5 0.7 maximum_maximum_fusion.w_ref
  5.2 0.8 multiply_select_fusion
  6.0 0.1 broadcast_bitcast_fusion
  6.1 0.9 copy.19.bias_ref
  7.0 3.9 %prep.1 = (bf16[4,16,16,1152]{3,2,1,0:T(8,128)(2,1)}, bf16[4,16,1152]{2,1,0:T(8,128)(2,1)}, bf16[4,1152]{1,0:T(4,128)(2,1)}) custom-call(f32[24,256]{1,0:T(8,128)} %maximum_maximum_fusion.w_ref, bf16[16,16,1152]{2,1,0:T(8,128)(2,1)} %k_ref.1, bf16[16,16,1152]{2,1,0:T(8,128)(2,1)} %v_ref.1, bf16[16,16,1152]{2,1,0:T(8,128)(2,1)} %kt_ref.1, ...), custom_call_target="tpu_custom_call" | custom-call | tf_op jit(solution)/shard_map/prep/pallas_call | solution.py:406
  10.9 180.9 %focal.1 = (bf16[16,16,1152]{2,1,0:T(8,128)(2,1)}, bf16[16,16,1152]{2,1,0:T(8,128)(2,1)}) custom-call(bf16[4,16,2,8,1152]{4,3,2,1,0:T(8,128)(2,1)} %bitcast.8, bf16[4,2,8,1152]{3,2,1,0:T(8,128)(2,1)} %bitcast.9, bf16[4,1152]{1,0:T(4,128)(2,1)} %get-tuple-element.7.far_in, bf16[16,16,1152]{2,1,0:T(8,128)(2,1)} %q_in.1, bf16[16,16,1152]{2,1,0:T(8,128)(2,1)} %qt_in.1, ...), custom_call_target="tpu_custom_call" | custom-call | tf_op jit(solution)/shard_map/focal/pallas_call | solution.py:418
  191.8 1.9 copy.22
  193.7 1.9 copy.23
  (1 shorter events, 0.0 us)

commit v3 on v2

v3 whole, which is shorter than its diff:
```python
import functools
import math

import jax
import jax.numpy as jnp
from jax import lax
from jax.experimental import pallas as pl
from jax.experimental.pallas import tpu as pltpu
from jax.sharding import PartitionSpec as P

HEADS = 16
HEAD_DIM = 72
D = 1152
WIN = 16
CELLS = WIN * WIN
NX, NY, NZ = 4, 4, 16
CHUNKS = D // 128
AHEAD = 2
MESH = pl.DeviceIdType.MESH
LOG2E = math.log2(math.e)
SCALE = HEAD_DIM**-0.5
NEG = -1e30

OWN, TOP, BOTTOM, LEFT, RIGHT = 0, 32, 48, 64, 80
TL, TR, BL, BR = 96, 104, 112, 120
NEAR, PAD, FAR = 128, 136, 144
GROUPS = 208
KEYS = GROUPS * 8
BLOCK = 32


def place():
    r, c = lax.axis_index("row"), lax.axis_index("col")
    y, x = r // 8, lax.rem(r, 4)
    z = lax.rem(r // 4, 2) * 8 + c // 2
    return r, c, x, y, z, lax.rem(c, 2)


def device(x, y, z, core):
    return (y * 8 + (z // 8) * 4 + x, lax.rem(z, 8) * 2 + core)


def main_kernel(
    k_in, v_in, kt_in, vt_in, q_in, qt_in, pool_near, pool_far, level_bias,
    mix_ref, tan_ref,
    keys, zbuf, relay, q_ref, qt_ref, s_ref, t_ref, w_ref, row_ref, sum_ref, mix_acc, tan_acc,
    halo_send, halo_recv, relay_send, relay_recv, misc_send, misc_recv, local_sem,
):
    r, c, x, y, z, core = place()
    fields = (k_in, v_in, kt_in, vt_in)
    up, down, west, east = r > 0, r < 31, c > 0, c < 15
    z_peers = [lax.rem(z + k, NZ) for k in range(1, NZ)]
    x_peers = [lax.rem(x + k, NX) for k in range(1, NX)]
    y_peers = [lax.rem(y + k, NY) for k in range(1, NY)]
    x_near = x + 1 - 2 * lax.rem(x, 2)
    near_peers = [device(x_near, y, z, core), device(x, y, z, 1 - core), device(x_near, y, z, 1 - core)]

    def lanes(chunk, count=1):
        return pl.ds(pl.multiple_of(chunk * 128, 128), count * 128)

    def part(first, count, chunk=None, width=1):
        return keys.at[:, pl.ds(first, count), :, slice(None) if chunk is None else lanes(chunk, width)]

    def drained(ref, sem):
        pltpu.make_async_copy(ref, ref, sem).wait()

    place_x = lax.rem(r, 4)
    far_down, far_up = down & (place_x == 3), up & (place_x == 0)
    hops = jnp.where(place_x >= 2, 2, -2)
    paired = (r + hops >= 0) & (r + hops < 32)
    relays_down, relays_up = paired & (place_x == 2), paired & (place_x == 1)

    def cut(rows, half, chunk):
        return [field.at[rows, half, :, lanes(chunk)] for field in fields]

    def strips(chunk):
        low = [cut(pl.ds(8, 8), half, chunk) for half in range(2)]
        high = [cut(pl.ds(0, 8), half, chunk) for half in range(2)]
        return [
            (down, low[0], TOP, 8, (r + 1, c), up),
            (up, high[0], BOTTOM, 8, (r - 1, c), down),
            (down & (place_x != 3), low[1], TOP + 8, 8, (r + 1, c), up),
            (up & (place_x != 0), high[1], BOTTOM + 8, 8, (r - 1, c), down),
        ]

    def relay_in(chunk, what):
        arrived = relay.at[:, :, :, lanes(chunk)]
        for n, cond, row, target in ((2, far_down, 8, (r - 1, c)), (3, far_up, 0, (r + 1, c))):
            slot = chunk * 10 + n

            @pl.when(cond)
            def _(row=row, target=target, slot=slot):
                if what == "start":
                    for f, src in enumerate(cut(pl.ds(row, 8), 1, chunk)):
                        pltpu.make_async_remote_copy(
                            src_ref=src, dst_ref=relay.at[f, :, :, lanes(chunk)],
                            send_sem=halo_send.at[slot], recv_sem=relay_recv.at[chunk],
                            device_id=target, device_id_type=MESH,
                        ).start()
                else:
                    drained(arrived, halo_send.at[slot])

    def relay_out(chunk, what):
        for n, cond, first, row in ((2, relays_down, TOP + 8, r + 2), (3, relays_up, BOTTOM + 8, r - 2)):
            copy = pltpu.make_async_remote_copy(
                src_ref=relay.at[:, :, :, lanes(chunk)], dst_ref=part(first, 8, chunk),
                send_sem=relay_send.at[chunk], recv_sem=halo_recv.at[chunk * 10 + n],
                device_id=(row, c), device_id_type=MESH,
            )
            if what == "start":
                arrived = relay.at[:, :, :, lanes(chunk)]

                @pl.when(cond)
                def _(copy=copy, arrived=arrived):
                    drained(arrived, relay_recv.at[chunk])
                    copy.start()
            else:
                pl.when(cond)(copy.wait_send)

    def sides(chunk):
        return [
            (east, cut(slice(None), 1, chunk), LEFT, 16, (r, c + 1), west),
            (west, cut(slice(None), 0, chunk), RIGHT, 16, (r, c - 1), east),
        ]

    def corners(chunk):
        return [
            (up & east, part(TOP + 8, 8, chunk), TL, 8, (r, c + 1), up & west),
            (up & west, part(TOP, 8, chunk), TR, 8, (r, c - 1), up & east),
            (down & east, part(BOTTOM + 8, 8, chunk), BL, 8, (r, c + 1), down & west),
            (down & west, part(BOTTOM, 8, chunk), BR, 8, (r, c - 1), down & east),
        ]

    def run(make, base, chunk, what):
        for n, (sends, src, first, count, target, receives) in enumerate(make(chunk)):
            slot = chunk * 10 + base + n
            whole = part(first, count, chunk)
            pairs = [(src, whole)]
            if isinstance(src, list):
                pairs = [(one, keys.at[f, pl.ds(first, count), :, lanes(chunk)]) for f, one in enumerate(src)]

            def go(pairs=pairs, slot=slot, target=target):
                for one, dst in pairs:
                    pltpu.make_async_remote_copy(
                        src_ref=one, dst_ref=dst, send_sem=halo_send.at[slot], recv_sem=halo_recv.at[slot],
                        device_id=target, device_id_type=MESH,
                    ).start()

            if what == "start":
                pl.when(sends)(go)
            elif what == "recv":
                pl.when(receives)(functools.partial(drained, whole, halo_recv.at[slot]))
            else:
                pl.when(sends)(functools.partial(drained, whole, halo_send.at[slot]))

    def to(src, dst, slot, target):
        return pltpu.make_async_remote_copy(
            src_ref=src, dst_ref=dst, send_sem=misc_send.at[slot], recv_sem=misc_recv.at[slot],
            device_id=target, device_id_type=MESH,
        )

    near_slot = NEAR + 2 * (lax.rem(x, 2) * 2 + core)
    for f, field in enumerate(fields):
        for half in range(2):
            pltpu.make_async_copy(field.at[:, half], keys.at[f, pl.ds(OWN + 16 * half, 16)], local_sem.at[0]).start()
    local = [pltpu.make_async_copy(q_in, q_ref, local_sem.at[1]), pltpu.make_async_copy(qt_in, qt_ref, local_sem.at[2])]
    for copy in local:
        copy.start()

    barrier = pltpu.get_barrier_semaphore()

    def greet(target):
        pl.semaphore_signal(barrier, inc=1, device_id=target, device_id_type=MESH)

    for cond, target in ((down, (r + 1, c)), (up, (r - 1, c)), (east, (r, c + 1)), (west, (r, c - 1))):
        pl.when(cond)(functools.partial(greet, target))
    fixed = (
        [device(x, y, p, core) for p in z_peers]
        + [device(p, y, z, core) for p in x_peers]
        + [device(x, p, z, core) for p in y_peers]
        + [device(x, y, z, 1 - core), device(x_near, y, z, 1 - core)]
    )
    for target in fixed:
        greet(target)
    pl.when(paired)(functools.partial(greet, (r + hops, c)))
    def clear(first, count):
        keys[:, pl.ds(first, count)] = jnp.zeros((4, count, 8, D), jnp.bfloat16)

    clear(PAD, FAR - PAD)
    for present, first, count in ((up, TOP, 16), (down, BOTTOM, 16), (west, LEFT, 16), (east, RIGHT, 16)):
        pl.when(jnp.logical_not(present))(functools.partial(clear, first, count))
    for present, first in ((up & west, TL), (up & east, TR), (down & west, BL), (down & east, BR)):
        pl.when(jnp.logical_not(present))(functools.partial(clear, first, 8))

    cell = lax.broadcasted_iota(jnp.int32, (16, CELLS), 1)
    row, col = (cell >> 3) & 15, (cell >> 7) * 8 + (cell & 7)
    in_block = lax.broadcasted_iota(jnp.int32, (16, CELLS), 0) == (row >> 2) * 4 + (col >> 2)
    weights = jnp.zeros((16, CELLS), jnp.float32)
    for p in range(4):
        for q in range(4):
            weights = jnp.where(in_block & ((row & 3) == p) & ((col & 3) == q), pool_near[p, q], weights)
    weights = jnp.concatenate([weights, jnp.broadcast_to(pool_far[...], (16, CELLS))], axis=0)
    high = weights.astype(jnp.bfloat16)
    rest = weights - high.astype(jnp.float32)
    middle = rest.astype(jnp.bfloat16)
    lowest = (rest - middle.astype(jnp.float32)).astype(jnp.bfloat16)
    drained(part(OWN, 32), local_sem.at[0])
    far_rows = []
    for f in range(4):
        flat = keys[f, pl.ds(OWN, 32)].reshape(CELLS, D)
        pooled = jnp.dot(lowest, flat, preferred_element_type=jnp.float32)
        pooled += jnp.dot(middle, flat, preferred_element_type=jnp.float32)
        pooled += jnp.dot(high, flat, preferred_element_type=jnp.float32)
        keys[f, pl.ds(near_slot, 2)] = pooled[:16].astype(jnp.bfloat16).reshape(2, 8, D)
        far_rows.append(pooled[16:17])
    zbuf[z] = jnp.concatenate(far_rows, axis=0).astype(jnp.bfloat16)
    edges = sum(cond.astype(jnp.int32) for cond in (down, up, east, west, paired))
    pl.semaphore_wait(barrier, len(fixed) + edges)

    def each(first, last, act):
        def body(chunk, carry):
            act(chunk)
            return carry

        lax.fori_loop(first, last, body, 0)

    def start(chunk):
        run(strips, 0, chunk, "start")
        run(sides, 4, chunk, "start")

    each(0, 1, lambda chunk: relay_in(chunk, "start"))
    for p in z_peers:
        to(zbuf.at[z], zbuf.at[z], 0, device(x, y, p, core)).start()

    def first_chunks(chunk):
        pl.when(chunk > 0)(lambda: relay_in(chunk, "start"))
        start(chunk)

    each(0, AHEAD, first_chunks)
    for target in near_peers:
        to(part(near_slot, 2), part(near_slot, 2), 4, target).start()

    far_group = FAR + 32 * core + 8 * y + 2 * x
    drained(zbuf.at[pl.ds(0, NZ - 1)], misc_recv.at[0])
    for f in range(4):
        cells = jnp.concatenate([zbuf[n].astype(jnp.float32)[f : f + 1] for n in range(NZ)], axis=0)
        keys[f, pl.ds(far_group, 2)] = cells.astype(jnp.bfloat16).reshape(2, 8, D)
    for copy in local:
        copy.wait()
    for p in x_peers:
        to(part(far_group, 2), part(far_group, 2), 1, device(p, y, z, core)).start()
    each(AHEAD, CHUNKS, lambda chunk: relay_in(chunk, "start"))
    each(0, AHEAD, lambda chunk: relay_out(chunk, "start"))
    drained(part(FAR, 6), misc_recv.at[1])
    far_y, far_core = FAR + 32 * core + 8 * y, FAR + 32 * core
    groups = ((0, 3), (3, CHUNKS - 3))

    def send_y(n):
        for p in y_peers:
            to(part(far_y, 8, *groups[n]), part(far_y, 8, *groups[n]), 2 + n, device(x, p, z, core)).start()

    swaps = [
        to(part(far_core, 32, *span), part(far_core, 32, *span), 5 + n, device(x, y, z, 1 - core))
        for n, span in enumerate(groups)
    ]
    send_y(0)
    drained(part(FAR, 24, *groups[0]), misc_recv.at[2])
    swaps[0].start()
    send_y(1)

    def advance(chunk):
        run(strips, 0, chunk, "recv")
        run(corners, 6, chunk, "start")

        @pl.when(chunk + AHEAD < CHUNKS)
        def _():
            start(chunk + AHEAD)
            relay_out(chunk + AHEAD, "start")

    def landed(chunk):
        run(sides, 4, chunk, "recv")
        run(corners, 6, chunk, "recv")

    each(0, 2, advance)
    drained(part(FAR, 24, *groups[1]), misc_recv.at[3])
    swaps[1].start()
    drained(part(NEAR, 6), misc_recv.at[4])

    def load(f, tile, count):
        width = 128 * count
        return keys[f, :, :, pl.ds(pl.multiple_of(tile * 128, 128), width)].reshape(KEYS, width)

    def query(ref, tile, count):
        width = 128 * count
        return ref[:, :, pl.ds(pl.multiple_of(tile * 128, 128), width)].reshape(CELLS, width)

    def in_head(head, tile, count):
        lane = lax.broadcasted_iota(jnp.int32, (1, 128 * count), 1) + tile * 128 - head * HEAD_DIM
        return (lane >= 0) & (lane < HEAD_DIM)

    def nt(a, b):
        return lax.dot_general(a, b, (((1,), (1,)), ((), ())), preferred_element_type=jnp.float32)

    def nn(a, b):
        return jnp.dot(a, b, preferred_element_type=jnp.float32)

    def tiles():
        return [slice(tile * 128, tile * 128 + 128) for tile in range(KEYS // 128)]

    def spread(column):
        return jnp.broadcast_to(column, (CELLS, 128))

    def gone(present):
        return jnp.where(present, 0.0, NEG).astype(jnp.float32)

    def put_scores(head, scores, tangent):
        near_bias, far_bias = level_bias[0, head] * LOG2E, level_bias[1, head] * LOG2E
        left_half = lax.broadcasted_iota(jnp.int32, (1, 128), 1) < 64
        offsets = [None, None, gone(up), gone(down), gone(west), gone(east)]
        offsets.append(jnp.where(left_half, gone(up & west), gone(up & east)))
        offsets.append(jnp.where(left_half, gone(down & west), gone(down & east)))
        offsets.append(jnp.where(left_half, near_bias, NEG))
        top = None
        for n, cols in enumerate(tiles()):
            scaled = scores[:, cols] * (SCALE * LOG2E)
            offset = offsets[n] if n < len(offsets) else far_bias
            scaled = scaled if offset is None else scaled + offset
            s_ref[:, cols] = scaled
            t_ref[:, cols] = tangent[:, cols] * SCALE
            top = scaled if top is None else jnp.maximum(top, scaled)
        row_ref[...] = spread(jnp.max(top, axis=1, keepdims=True))

    def softmax():
        def exponentials(n, carry):
            rows = pl.ds(pl.multiple_of(n * BLOCK, BLOCK), BLOCK)
            top = row_ref[rows, :]
            total = None
            for cols in tiles():
                expd = jnp.exp2(s_ref[rows, cols] - top)
                s_ref[rows, cols] = expd
                total = expd if total is None else total + expd
            sum_ref[rows, :] = total
            return carry

        def products(n, carry):
            rows = pl.ds(pl.multiple_of(n * BLOCK, BLOCK), BLOCK)
            late = pl.ds(pl.multiple_of(CELLS + n * BLOCK, BLOCK), BLOCK)
            inverse = row_ref[rows, :]
            total = None
            for cols in tiles():
                weights = s_ref[rows, cols] * inverse
                product = weights * t_ref[rows, cols]
                w_ref[rows, cols] = weights.astype(jnp.bfloat16)
                w_ref[late, cols] = product.astype(jnp.bfloat16)
                total = product if total is None else total + product
            sum_ref[rows, :] = total
            return carry

        lax.fori_loop(0, CELLS // BLOCK, exponentials, 0)
        row_ref[...] = spread(1.0 / jnp.sum(sum_ref[...], axis=1, keepdims=True))
        lax.fori_loop(0, CELLS // BLOCK, products, 0)

    def finish(head, tile, count, mix, product_mix, weight_tan):
        cols = pl.ds(pl.multiple_of(tile * 128, 128), 128 * count)
        keep = in_head(head, tile, count)
        row_total = jnp.sum(sum_ref[...], axis=1, keepdims=True)
        mix_tan = product_mix + weight_tan - row_total * mix
        mix_acc[:, cols] = jnp.where(keep, mix, mix_acc[:, cols])
        tan_acc[:, cols] = jnp.where(keep, mix_tan, tan_acc[:, cols])

    def step(n, carry):
        late = (n >= 4).astype(jnp.int32)
        head, tile = 2 * n + late, n + late
        mask = in_head(head, tile, 1).astype(jnp.float32).astype(jnp.bfloat16)
        q = query(q_ref, tile, 1) * mask
        qt = query(qt_ref, tile, 1) * mask
        both = jnp.concatenate([jnp.concatenate([q, jnp.zeros_like(q)], 1), jnp.concatenate([qt, q], 1)], 0)
        scores = nt(both, jnp.concatenate([load(0, tile, 1), load(2, tile, 1)], 1))
        put_scores(head, scores[:CELLS], scores[CELLS:])
        softmax()
        mixed = nn(w_ref[...], jnp.concatenate([load(1, tile, 1), load(3, tile, 1)], 1))
        finish(head, tile, 1, mixed[:CELLS, :128], mixed[CELLS:, :128], mixed[:CELLS, 128:])
        head, tile = 2 * n + 1 - late, n
        mask = in_head(head, tile, 2).astype(jnp.float32).astype(jnp.bfloat16)
        q = query(q_ref, tile, 2) * mask
        qt = query(qt_ref, tile, 2) * mask
        scores = nt(jnp.concatenate([q, qt], 0), load(0, tile, 2))
        put_scores(head, scores[:CELLS], scores[CELLS:] + nt(q, load(2, tile, 2)))
        softmax()
        mixed = nn(w_ref[...], load(1, tile, 2))
        finish(head, tile, 2, mixed[:CELLS], mixed[CELLS:], nn(w_ref[pl.ds(0, CELLS), :], load(3, tile, 2)))
        return carry

    swaps[0].wait_recv()
    landed(0)

    def chunk_step(n, carry):
        pl.when(n + 2 < CHUNKS)(lambda: advance(n + 2))
        pl.when(n == 2)(swaps[1].wait_recv)
        landed(n + 1)
        return step(n, carry)

    lax.fori_loop(0, HEADS // 2, chunk_step, 0)
    mix_ref[...] = mix_acc[...].astype(jnp.bfloat16).reshape(WIN, WIN, D)
    tan_ref[...] = tan_acc[...].astype(jnp.bfloat16).reshape(WIN, WIN, D)

    def sent(chunk):
        run(strips, 0, chunk, "sent")
        run(sides, 4, chunk, "sent")
        run(corners, 6, chunk, "sent")
        relay_in(chunk, "sent")
        relay_out(chunk, "sent")

    each(0, CHUNKS, sent)
    drained(zbuf.at[pl.ds(0, NZ - 1)], misc_send.at[0])
    drained(part(FAR, 6), misc_send.at[1])
    for n, span in enumerate(groups):
        drained(part(FAR, 24, *span), misc_send.at[2 + n])
        swaps[n].wait_send()
    drained(part(NEAR, 6), misc_send.at[4])


def body(query_field, key_field, value_field, query_tan, key_tan, value_tan, pool_near, pool_far, level_bias):
    vmem = pl.BlockSpec(memory_space=pltpu.VMEM)
    smem = pl.BlockSpec(memory_space=pltpu.SMEM)
    anywhere = pl.BlockSpec(memory_space=pl.ANY)
    field = jax.ShapeDtypeStruct((WIN, WIN, D), jnp.bfloat16)
    halo = 10 * CHUNKS
    return pl.pallas_call(
        main_kernel,
        out_shape=(field, field),
        in_specs=[anywhere] * 6 + [smem, vmem, smem],
        out_specs=(vmem, vmem),
        scratch_shapes=[
            pltpu.VMEM((4, GROUPS, 8, D), jnp.bfloat16),
            pltpu.VMEM((NZ, 4, D), jnp.bfloat16),
            pltpu.VMEM((4, 8, 8, D), jnp.bfloat16),
            pltpu.VMEM((WIN, WIN, D), jnp.bfloat16),
            pltpu.VMEM((WIN, WIN, D), jnp.bfloat16),
            pltpu.VMEM((CELLS, KEYS), jnp.float32),
            pltpu.VMEM((CELLS, KEYS), jnp.float32),
            pltpu.VMEM((2 * CELLS, KEYS), jnp.bfloat16),
            pltpu.VMEM((CELLS, 128), jnp.float32),
            pltpu.VMEM((CELLS, 128), jnp.float32),
            pltpu.VMEM((CELLS, D), jnp.float32),
            pltpu.VMEM((CELLS, D), jnp.float32),
            pltpu.SemaphoreType.DMA((halo,)),
            pltpu.SemaphoreType.DMA((halo,)),
            pltpu.SemaphoreType.DMA((CHUNKS,)),
            pltpu.SemaphoreType.DMA((CHUNKS,)),
            pltpu.SemaphoreType.DMA((7,)),
            pltpu.SemaphoreType.DMA((7,)),
            pltpu.SemaphoreType.DMA((3,)),
        ],
        compiler_params=pltpu.CompilerParams(
            collective_id=0, has_side_effects=True, vmem_limit_bytes=60 * 1024 * 1024
        ),
        name="focal",
    )(
        *(field.reshape(WIN, 2, 8, D) for field in (key_field, value_field, key_tan, value_tan)),
        query_field, query_tan, pool_near,
        pool_far.reshape(WIN, 2, 8).transpose(1, 0, 2).reshape(1, CELLS), level_bias,
    )


def solution(mesh):
    spec = P("row", "col", None)
    return jax.shard_map(
        body, mesh=mesh, in_specs=(spec,) * 6 + (P(),) * 3, out_specs=(spec, spec), check_vma=False
    )
```

time: 196 us -> 144 us (0.73)
  the two profiles are of different devices: /device:TPU:68 before, /device:TPU:25 now
where the time goes in v3:
time: 144 us; the launch traced here: 142 us
  Pallas kernels  137 us (95%)
  local copies, waits for them, and re-layouts  4.3 us (3%)
    pallas_call x1, Pallas kernels, body(): pl.pallas_call(main_kernel, out_shape=(field, field), in_specs=[anywhere]...  137 us
    unnamed x5, local copies, waits for them, and re-layouts  3.57 us

profile of v3, /device:TPU:25, one launch (start us, length us, event | category | flops | bytes accessed | tf_op | source)
XLA Modules:
  0.0 142.2 jit_solution(16940483725129060749)
XLA Ops:
  0.6 0.8 copy.12
  1.4 0.1 copy.13
  1.5 0.7 reshape.27.pool_far
  2.1 137.2 %focal.1 = (bf16[16,16,1152]{2,1,0:T(8,128)(2,1)}, bf16[16,16,1152]{2,1,0:T(8,128)(2,1)}) custom-call(bf16[16,2,8,1152]{3,2,1,0:T(8,128)(2,1)} %bitcast.7, bf16[16,2,8,1152]{3,2,1,0:T(8,128)(2,1)} %bitcast.8, bf16[16,2,8,1152]{3,2,1,0:T(8,128)(2,1)} %bitcast.9, bf16[16,2,8,1152]{3,2,1,0:T(8,128)(2,1)} %bitcast.10, bf16[16,16,1152]{2,1,0:T(8,128)(2,1)} %q_in.1, ...), custom_call_target="tpu_custom_call" | custom-call | tf_op jit(solution)/shard_map/focal/pallas_call | solution.py:429
  139.4 0.0 copy-start
  139.4 2.0 %copy.16 = bf16[16,16,1152]{2,1,0:T(8,128)(2,1)} copy(bf16[16,16,1152]{2,1,0:T(8,128)(2,1)} %get-tuple-element.4) | data formatting | bytes 1179648
  141.4 0.0 copy-done
  141.4 0.8 copy.17
Async XLA Ops:
  139.4 2.0 %copy-start = (bf16[16,16,1152]{2,1,0:T(8,128)(2,1)S(1)}, bf16[16,16,1152]{2,1,0:T(8,128)(2,1)}, u32[]{:S(2)}) copy-start(bf16[16,16,1152]{2,1,0:T(8,128)(2,1)} %get-tuple-element.5) | copy-start | bytes 1769476

commit v4 on v3

--- a/solution.py
+++ b/solution.py
@@ -26,7 +26,7 @@
 NEAR, PAD, FAR = 128, 136, 144
 GROUPS = 208
 KEYS = GROUPS * 8
-BLOCK = 32
+BLOCK = 64
 
 
 def place():
@@ -264,10 +264,6 @@
         for n, span in enumerate(groups)
     ]
     send_y(0)
-    drained(part(FAR, 24, *groups[0]), misc_recv.at[2])
-    swaps[0].start()
-    send_y(1)
-
     def advance(chunk):
         run(strips, 0, chunk, "recv")
         run(corners, 6, chunk, "start")
@@ -281,7 +277,12 @@
         run(sides, 4, chunk, "recv")
         run(corners, 6, chunk, "recv")
 
-    each(0, 2, advance)
+    each(0, 1, advance)
+    drained(part(FAR, 24, *groups[0]), misc_recv.at[2])
+    swaps[0].start()
+    send_y(1)
+
+    each(1, 2, advance)
     drained(part(FAR, 24, *groups[1]), misc_recv.at[3])
     swaps[1].start()
     drained(part(NEAR, 6), misc_recv.at[4])

time: 144 us -> 142 us (0.986); the launches traced: 142 us -> 142 us
  no operation moved by 1% of the time
where the time goes in v4:
time: 142 us
  Pallas kernels  137 us (96%)
  local copies, waits for them, and re-layouts  4.3 us (3%)
    pallas_call x1, Pallas kernels, body(): pl.pallas_call(main_kernel, out_shape=(field, field), in_specs=[anywhere]...  137 us
    unnamed x5, local copies, waits for them, and re-layouts  3.57 us

profile of v4, /device:TPU:25, one launch (start us, length us, event | category | flops | bytes accessed | tf_op | source)
XLA Modules:
  0.0 142.1 jit_solution(5644922308666639537)
XLA Ops:
  0.6 0.8 copy.12
  1.4 0.1 copy.13
  1.5 0.7 reshape.27.pool_far
  2.1 137.2 %focal.1 = (bf16[16,16,1152]{2,1,0:T(8,128)(2,1)}, bf16[16,16,1152]{2,1,0:T(8,128)(2,1)}) custom-call(bf16[16,2,8,1152]{3,2,1,0:T(8,128)(2,1)} %bitcast.7, bf16[16,2,8,1152]{3,2,1,0:T(8,128)(2,1)} %bitcast.8, bf16[16,2,8,1152]{3,2,1,0:T(8,128)(2,1)} %bitcast.9, bf16[16,2,8,1152]{3,2,1,0:T(8,128)(2,1)} %bitcast.10, bf16[16,16,1152]{2,1,0:T(8,128)(2,1)} %q_in.1, ...), custom_call_target="tpu_custom_call" | custom-call | tf_op jit(solution)/shard_map/focal/pallas_call | solution.py:430
  139.3 0.0 copy-start
  139.3 2.0 %copy.16 = bf16[16,16,1152]{2,1,0:T(8,128)(2,1)} copy(bf16[16,16,1152]{2,1,0:T(8,128)(2,1)} %get-tuple-element.4) | data formatting | bytes 1179648
  141.3 0.0 copy-done
  141.3 0.8 copy.17
Async XLA Ops:
  139.3 2.0 %copy-start = (bf16[16,16,1152]{2,1,0:T(8,128)(2,1)S(1)}, bf16[16,16,1152]{2,1,0:T(8,128)(2,1)}, u32[]{:S(2)}) copy-start(bf16[16,16,1152]{2,1,0:T(8,128)(2,1)} %get-tuple-element.5) | copy-start | bytes 1769476
